TPU v7x, 256 devices: a whole 4x4x8 slice. The times are simulated.
256 devices in a mesh: cuts: 8 (over x_lo, y), gz: 32 (over z, x_hi, core).
Axes of the slice: x: 4 (x_hi: 2, x_lo: 2; x = x_hi * 2 + x_lo), y: 4, z: 8, core: 2. Of those that a mesh axis runs over, the one named last changes fastest.
Arguments:
- vectors: float32 [8, 32, 64, 128, 128], P('cuts', None, 'gz'), may hold values from -9 to 9
- onsite: float32 [64, 128, 128], P('gz'), may hold values from -8.25 to 8.25
- center: float32 [8], P('cuts'), may hold values from -3 to 3
- inv_half: float32 [8], P('cuts'), may hold values from 0.06 to 0.1
- cheb_coef: float32 [8, 3], P('cuts'), may hold values from 0.5 to 1.5
Outputs:
- basis: float32 [8, 64, 64, 128, 128], P('cuts', None, 'gz')
- projected: float32 [8, 64, 64], P('cuts')
All inputs are finite; a program needn't handle non-finite values.
Results may differ from a plain program's by a relative error of at most 0.00018.
Values sent between devices are 32-bit elements; how exact they have to be, the bound alone decides.
A program may use at most 128 MiB of HBM per device.

v0:
```python
import jax
import jax.numpy as jnp
from jax import lax
from jax.sharding import PartitionSpec as P


def padded_2(array, sides, width):
    for axis, dim in sides:
        size, length = (lax.axis_size(axis), array.shape[dim])
        up = [(i, (i + 1) % size) for i in range(size)]
        down = [(j, i) for i, j in up]
        last = lax.slice_in_dim(array, length - width, length, axis=dim)
        leading = lax.slice_in_dim(array, 0, width, axis=dim)
        before = lax.ppermute(last, axis, up)
        after = lax.ppermute(leading, axis, down)
        array = jnp.concatenate([before, array, after], axis=dim)
    return array


def from_behind(block, axis, distance):
    devices = range(lax.axis_size(axis))
    route = [(i - distance, i) for i in devices if i - distance in devices]
    return lax.ppermute(block, axis, route)


def neighbours_xy(middle):
    padded = jnp.pad(middle, ((0, 0), (0, 0), (1, 1), (1, 1)))
    return (
        padded[:, :, 2:, 1:-1]
        + padded[:, :, :-2, 1:-1]
        + padded[:, :, 1:-1, 2:]
        + padded[:, :, 1:-1, :-2]
    )


def hamiltonian(extended, onsite_part):
    middle = extended[:, 1:-1]
    along_z = extended[:, 2:] + extended[:, :-2]
    return onsite_part[None] * middle - along_z - neighbours_xy(middle)


def product(left, right):
    return jnp.dot(left, right, precision=lax.Precision.HIGHEST, preferred_element_type=jnp.float32)


def body(vectors, onsite, center, inv_half, cheb_coef):
    field = vectors[0]
    count = field.shape[0]
    layers = field.shape[1]
    sites_all = layers * lax.axis_size("gz") * field.shape[2] * field.shape[3]
    identity = jnp.eye(2 * count, dtype=jnp.float32)

    def scaled(extended, onsite_part):
        return inv_half[0] * (hamiltonian(extended, onsite_part) - center[0] * extended[:, 1:-1])

    def filter_step(values):
        return padded_2(values, (("gz", 1),), 1)

    first = scaled(filter_step(field), onsite)
    second = 2.0 * scaled(filter_step(first), onsite) - field
    filtered = cheb_coef[0, 0] * field + cheb_coef[0, 1] * first + cheb_coef[0, 2] * second
    partner = from_behind(filtered, "cuts", -1)
    union = jnp.concatenate([filtered, partner], 0).reshape(2 * count, -1)
    gram = lax.psum(product(union, union.T), "gz") / sites_all + 0.25 * identity
    factor = jnp.linalg.cholesky(gram)
    inverse = jax.scipy.linalg.solve_triangular(factor, identity, lower=True)
    basis = product(inverse, union)
    shaped = basis.reshape(2 * count, layers, field.shape[2], field.shape[3])
    images = hamiltonian(padded_2(shaped, (("gz", 1),), 1), onsite).reshape(2 * count, -1)
    projected = lax.psum(product(basis, images.T), "gz") / sites_all
    return (basis.reshape(1, 2 * count, layers, field.shape[2], field.shape[3]), projected[None])


def solution(mesh):
    in_specs = (
        P("cuts", None, "gz", None, None),
        P("gz", None, None),
        P("cuts"),
        P("cuts"),
        P("cuts", None),
    )
    out_specs = (P("cuts", None, "gz", None, None), P("cuts", None, None))
    return jax.shard_map(body, mesh=mesh, in_specs=in_specs, out_specs=out_specs, check_vma=False)
```

profile of v0, /device:TPU:24, one launch (start us, length us, event | category | flops | bytes accessed | tf_op | source)
XLA Modules:
  0.0 651.8 jit_solution(12368654120373299613)
XLA Ops:
  0.6 4.6 copy.28
  5.7 7.8 %collective-permute-start = (f32[32,1,128,128]{3,0,2,1:T(8,128)S(1)}, f32[32,1,128,128]{3,0,2,1:T(8,128)S(1)}, u32[]{:S(2)}, u32[]{:S(2)}) collective-permute-start(f32[32,1,128,128]{3,0,2,1:T(8,128)S(1)} %get-tuple-element.6), channel_id=1, source_target_pairs={{1,0},{2,1},{3,2},{4,3},{5,4},{6,5},{7,6},{8,7},{9,8},{10,9},{11,1... | collective-permute-start | bytes 6291464 | tf_op jit(solution)/shard_map/ppermute | solution.py:15
  14.8 22.3 %collective-permute-done = f32[32,1,128,128]{3,0,2,1:T(8,128)S(1)} collective-permute-done((f32[32,1,128,128]{3,0,2,1:T(8,128)S(1)}, f32[32,1,128,128]{3,0,2,1:T(8,128)S(1)}, u32[]{:S(2)}, u32[]{:S(2)}) %collective-permute-start) | collective-permute-done | bytes 2097184 | tf_op jit(solution)/shard_map/ppermute | solution.py:15
  37.1 5.6 collective-permute-done.1
  42.7 3.5 fusion.17
  46.8 34.3 %collective-permute-start.3 = (f32[32,1,128,128]{3,0,2,1:T(8,128)S(1)}, f32[32,1,128,128]{3,0,2,1:T(8,128)S(1)}, u32[]{:S(2)}, u32[]{:S(2)}) collective-permute-start(f32[32,1,128,128]{3,0,2,1:T(8,128)S(1)} %get-tuple-element.5), channel_id=1, source_target_pairs={{0,1},{1,2},{2,3},{3,4},{4,5},{5,6},{6,7},{7,8},{8,9},{9,10},{10,1... | collective-permute-start | bytes 6291464 | tf_op jit(solution)/shard_map/ppermute | solution.py:14
  81.1 0.7 fusion.39
  81.7 2.9 collective-permute-done.2
  84.6 29.4 %collective-permute-done.3 = f32[32,1,128,128]{3,0,2,1:T(8,128)S(1)} collective-permute-done((f32[32,1,128,128]{3,0,2,1:T(8,128)S(1)}, f32[32,1,128,128]{3,0,2,1:T(8,128)S(1)}, u32[]{:S(2)}, u32[]{:S(2)}) %collective-permute-start.3) | collective-permute-done | bytes 2097184 | tf_op jit(solution)/shard_map/ppermute | solution.py:14
  114.1 1.3 copy-done.4
  115.4 9.1 %fusion.27 = f32[32,2,128,128]{3,0,2,1:T(8,128)S(1)} fusion(f32[32,2,128,128]{3,0,2,1:T(8,128)S(1)} %fusion.17, f32[32,1,128,128]{3,0,2,1:T(8,128)} %copy-done.4, f32[32,1,128,128]{3,0,2,1:T(8,128)S(1)} %collective-permute-done.2, f32[]{:T(128)} %bitcast.5, f32[]{:T(128)} %bitcast.44, f32[2,128,128]{2,1,0:T(8,128)S(1)} %copy-done.5, f32[]{:T(128)} %bitcast.46, ...), kind=kLoop, calls=%fused_computation.42 | loop fusion | flops 19922944 | bytes 16908308 | tf_op jit(solution)/shard_map/add | solution.py:61
  124.5 2.9 collective-permute-start.4
  127.5 74.5 %collective-permute-done.4 = f32[32,2,128,128]{3,0,2,1:T(8,128)S(1)} collective-permute-done((f32[32,2,128,128]{3,0,2,1:T(8,128)S(1)}, f32[32,2,128,128]{3,0,2,1:T(8,128)S(1)}, u32[]{:S(2)}, u32[]{:S(2)}) %collective-permute-start.4) | collective-permute-done | bytes 4194336 | tf_op jit(solution)/shard_map/ppermute | solution.py:23
  202.0 2.0 copy-done.3
  204.0 6.6 %convolution_bitcast_fusion = f32[64,64]{1,0:T(8,128)S(1)} fusion(f32[32,2,128,128]{3,0,2,1:T(8,128)S(1)} %collective-permute-done.4, f32[32,2,128,128]{3,0,2,1:T(8,128)S(1)} %fusion.27), kind=kOutput, calls=%fused_computation.52 | convolution fusion | flops 1612709888 | bytes 8404992 | tf_op jit(solution)/shard_map/dot_general | solution.py:43
  210.6 149.8 %psum.14 = f32[64,64]{1,0:T(8,128)S(1)} all-reduce(f32[64,64]{1,0:T(8,128)S(1)} %convolution_bitcast_fusion), channel_id=1, replica_groups=mesh['cuts'=8,'gz'=32] {'gz'}, use_global_device_ids=true, to_apply=%region_0.1 | all-reduce | flops 4096 | bytes 32768 | tf_op jit(solution)/shard_map/psum | solution.py:64
  360.5 4.5 pad_maximum_fusion.2
  365.0 8.3 %copy.11 = f32[64,2,128,128]{3,2,1,0:T(8,128)} copy(f32[64,2,128,128]{3,0,2,1:T(8,128)S(1)} %pad_maximum_fusion.2) | data formatting | bytes 16777216 | tf_op jit(solution)/shard_map/concatenate | solution.py:63
  373.4 5.8 cholesky.17
  379.3 0.6 compare_reduce_fusion
  379.9 0.7 fusion.32
  380.6 4.9 custom-call.7
  385.7 16.2 %fusion.7 = f32[64,32768]{1,0:T(8,128)S(1)} fusion(f32[64,64]{1,0:T(8,128)S(1)} %fusion.33, f32[8,8,256,128]{3,2,1,0:T(8,128)} %bitcast.54), kind=kOutput, calls=%fused_computation.19 | convolution fusion | flops 1610612736 | bytes 16793600 | tf_op jit(solution)/shard_map/dot_general | solution.py:43
  401.9 1.5 copy.14
  403.4 4.2 fusion.36
  407.6 0.5 collective-permute-start.6
  408.1 45.9 %collective-permute-done.5 = f32[64,1,128,128]{3,2,1,0:T(8,128)} collective-permute-done((f32[64,1,128,128]{3,2,1,0:T(8,128)}, f32[64,1,128,128]{3,2,1,0:T(8,128)}, u32[]{:S(2)}, u32[]{:S(2)}) %collective-permute-start.5) | collective-permute-done | bytes 4194336 | tf_op jit(solution)/shard_map/ppermute | solution.py:15
  454.0 5.6 collective-permute-done.6
  459.6 10.0 %fusion.3 = f32[64,2,128,128]{3,2,1,0:T(8,128)} fusion(f32[64,2,128,128]{3,2,1,0:T(8,128)S(1)} %bitcast.48, f32[64,1,128,128]{3,2,1,0:T(8,128)} %collective-permute-done.6, f32[64,1,128,128]{3,2,1,0:T(8,128)} %collective-permute-done.5, f32[2,128,128]{2,1,0:T(8,128)S(1)} %copy-done.5), kind=kLoop, calls=%fused_computation.15 | loop fusion | flops 18874368 | bytes 25296896 | tf_op jit(solution)/shard_map/sub | solution.py:39
  469.5 15.6 %fusion.4 = f32[64,64]{1,0:T(8,128)S(1)} fusion(f32[64,32768]{1,0:T(8,128)S(1)} %fusion.7, f32[8,8,256,128]{3,2,1,0:T(8,128)} %bitcast.53), kind=kOutput, calls=%fused_computation.16 | convolution fusion | flops 1610612736 | bytes 16793600 | tf_op jit(solution)/shard_map/dot_general | solution.py:43
  485.2 165.7 %psum.15 = f32[64,64]{1,0:T(8,128)S(1)} all-reduce(f32[64,64]{1,0:T(8,128)S(1)} %fusion.4), channel_id=1, replica_groups=mesh['cuts'=8,'gz'=32] {'gz'}, use_global_device_ids=true, to_apply=%region_3.4 | all-reduce | flops 4096 | bytes 32768 | tf_op jit(solution)/shard_map/psum | solution.py:70
  650.9 0.6 multiply_bitcast_fusion
  (22 shorter events, 1.4 us)
Async XLA Ops:
  5.2 37.5 %copy-start.5 = (f32[2,128,128]{2,1,0:T(8,128)S(1)}, f32[2,128,128]{2,1,0:T(8,128)}, u32[]{:S(2)}) copy-start(f32[2,128,128]{2,1,0:T(8,128)} %param.6) | copy-start | bytes 393220
  5.7 31.4 %collective-permute-start = (f32[32,1,128,128]{3,0,2,1:T(8,128)S(1)}, f32[32,1,128,128]{3,0,2,1:T(8,128)S(1)}, u32[]{:S(2)}, u32[]{:S(2)}) collective-permute-start(f32[32,1,128,128]{3,0,2,1:T(8,128)S(1)} %get-tuple-element.6), channel_id=1, source_target_pairs={{1,0},{2,1},{3,2},{4,3},{5,4},{6,5},{7,6},{8,7},{9,8},{10,9},{11,1... | collective-permute-start | bytes 6291464 | tf_op jit(solution)/shard_map/ppermute | solution.py:15
  13.5 29.2 %collective-permute-start.1 = (f32[32,1,128,128]{3,0,2,1:T(8,128)S(1)}, f32[32,1,128,128]{3,0,2,1:T(8,128)S(1)}, u32[]{:S(2)}, u32[]{:S(2)}) collective-permute-start(f32[32,1,128,128]{3,0,2,1:T(8,128)S(1)} %get-tuple-element.7), channel_id=1, source_target_pairs={{0,1},{1,2},{2,3},{3,4},{4,5},{5,6},{6,7},{7,8},{8,9},{9,10},{10,1... | collective-permute-start | bytes 6291464 | tf_op jit(solution)/shard_map/ppermute | solution.py:14
  46.2 34.9 %copy-start.6 = (f32[1,3]{1,0:T(1,128)S(1)}, f32[1,3]{1,0:T(1,128)}, u32[]{:S(2)}) copy-start(f32[1,3]{1,0:T(1,128)} %param.9) | copy-start | bytes 40
  46.2 69.2 %copy-start.2 = (f32[1,32,2,128,128]{4,3,2,1,0:T(8,128)S(1)}, f32[1,32,2,128,128]{4,3,2,1,0:T(8,128)}, u32[]{:S(2)}) copy-start(f32[1,32,2,128,128]{4,3,2,1,0:T(8,128)} %param.5) | copy-start | bytes 12582916
  46.7 38.0 %collective-permute-start.2 = (f32[32,1,128,128]{3,0,2,1:T(8,128)S(1)}, f32[32,1,128,128]{3,0,2,1:T(8,128)S(1)}, u32[]{:S(2)}, u32[]{:S(2)}) collective-permute-start(f32[32,1,128,128]{3,0,2,1:T(8,128)S(1)} %get-tuple-element.4), channel_id=1, source_target_pairs={{1,0},{2,1},{3,2},{4,3},{5,4},{6,5},{7,6},{8,7},{9,8},{10,9},{11,1... | collective-permute-start | bytes 6291464 | tf_op jit(solution)/shard_map/ppermute | solution.py:15
  46.8 67.3 %collective-permute-start.3 = (f32[32,1,128,128]{3,0,2,1:T(8,128)S(1)}, f32[32,1,128,128]{3,0,2,1:T(8,128)S(1)}, u32[]{:S(2)}, u32[]{:S(2)}) collective-permute-start(f32[32,1,128,128]{3,0,2,1:T(8,128)S(1)} %get-tuple-element.5), channel_id=1, source_target_pairs={{0,1},{1,2},{2,3},{3,4},{4,5},{5,6},{6,7},{7,8},{8,9},{9,10},{10,1... | collective-permute-start | bytes 6291464 | tf_op jit(solution)/shard_map/ppermute | solution.py:14
  114.0 1.3 copy-start.4
  124.5 77.5 %copy-start.1 = (f32[32,2,128,128]{3,0,2,1:T(8,128)}, f32[32,2,128,128]{3,0,2,1:T(8,128)S(1)}, u32[]{:S(2)}) copy-start(f32[32,2,128,128]{3,0,2,1:T(8,128)S(1)} %fusion.27) | copy-start | bytes 12582916
  124.5 77.5 %collective-permute-start.4 = (f32[32,2,128,128]{3,0,2,1:T(8,128)S(1)}, f32[32,2,128,128]{3,0,2,1:T(8,128)S(1)}, u32[]{:S(2)}, u32[]{:S(2)}) collective-permute-start(f32[32,2,128,128]{3,0,2,1:T(8,128)S(1)} %fusion.27), channel_id=1, source_target_pairs={{32,0},{64,32},{96,64},{128,96},{160,128},{192,160},{224,192},{33,... | collective-permute-start | bytes 12582920 | tf_op jit(solution)/shard_map/ppermute | solution.py:23
  202.0 2.0 copy-start.3
  403.4 56.1 %copy-start = (f32[8,8,256,128]{3,2,1,0:T(8,128)}, f32[8,8,256,128]{3,2,1,0:T(8,128)S(1)}, u32[]{:S(2)}) copy-start(f32[8,8,256,128]{3,2,1,0:T(8,128)S(1)} %copy.14) | copy-start | bytes 25165828
  407.6 46.4 %collective-permute-start.5 = (f32[64,1,128,128]{3,2,1,0:T(8,128)}, f32[64,1,128,128]{3,2,1,0:T(8,128)}, u32[]{:S(2)}, u32[]{:S(2)}) collective-permute-start(f32[64,1,128,128]{3,2,1,0:T(8,128)} %get-tuple-element.2), channel_id=1, source_target_pairs={{1,0},{2,1},{3,2},{4,3},{5,4},{6,5},{7,6},{8,7},{9,8},{10,9},{11,1... | collective-permute-start | bytes 12582920 | tf_op jit(solution)/shard_map/ppermute | solution.py:15
  407.6 52.0 %collective-permute-start.6 = (f32[64,1,128,128]{3,2,1,0:T(8,128)}, f32[64,1,128,128]{3,2,1,0:T(8,128)}, u32[]{:S(2)}, u32[]{:S(2)}) collective-permute-start(f32[64,1,128,128]{3,2,1,0:T(8,128)} %get-tuple-element.3), channel_id=1, source_target_pairs={{0,1},{1,2},{2,3},{3,4},{4,5},{5,6},{6,7},{7,8},{8,9},{9,10},{10,1... | collective-permute-start | bytes 12582920 | tf_op jit(solution)/shard_map/ppermute | solution.py:14
where the time goes:
time: 659 us; the launch traced here: 652 us
  blocking collectives  316 us (48%)
  waiting for transfers between devices  186 us (28%)
  starting transfers between devices  45.7 us (7%)
  other arithmetic  39.8 us (6%)
  matrix products  38.7 us (6%)
  local copies, waits for them, and re-layouts  23.5 us (4%)
    psum x1, blocking collectives, body(): projected = lax.psum(product(basis, images.T), 'gz') / sites_all  166 us
    psum x1, blocking collectives, body(): gram = lax.psum(product(union, union.T), 'gz') / sites_all + 0.25 * identity  150 us
    ppermute x1, waiting for transfers between devices, from_behind(): return lax.ppermute(block, axis, route)  74.5 us
    ppermute x3, waiting for transfers between devices, padded_2(): after = lax.ppermute(leading, axis, down)  71.1 us
    ppermute x3, waiting for transfers between devices, padded_2(): before = lax.ppermute(last, axis, up)  40.6 us
    dot_general x3, matrix products, product(): jnp.dot(left, right, precision=lax.Precision.HIGHEST, preferred_element_t...  38.5 us
    ppermute x3, starting transfers between devices, padded_2(): before = lax.ppermute(last, axis, up)  34.8 us
  transfers between devices with their start and end apart: 7, of which 7 were waited for; matrix products, arithmetic and copies ran while one was open for 0% of the time, Pallas kernels for 0%

commit v1 on v0

v1 whole, which is shorter than its diff:
```python
import functools

import jax
import jax.numpy as jnp
from jax import lax
from jax.experimental import pallas as pl
from jax.experimental.pallas import tpu as pltpu
from jax.sharding import PartitionSpec as P

MESH = pl.DeviceIdType.MESH
K = 32
LX = 128
LY = 128
XR = 8
NC = LX // XR
LAG = 2
N_CUTS = 8
N_GZ = 32
SITES = 64 * 128 * 128
F32 = jnp.float32
BF16 = jnp.bfloat16


def lanes(v):
    at = lax.broadcasted_iota(jnp.int32, v.shape, v.ndim - 1)
    left = jnp.where(at == 0, 0.0, pltpu.roll(v, 1, v.ndim - 1))
    right = jnp.where(at == LY - 1, 0.0, pltpu.roll(v, LY - 1, v.ndim - 1))
    return left + right


def filter_kernel(
    v_hbm, on_hbm, par, u_hbm, acc_ref,
    raw, vt, first, u, ops, acc, ons, relay,
    own_s, on_s, on_r, up_s, up_r, dn_s, dn_r, far_s, far_r, fwd_s, y_s, y_r,
    rel_s, rel_r, gf_s, gf_r, out_s,
):
    c = lax.axis_index("cuts")
    g = lax.axis_index("gz")
    k = lax.rem(g, 2)
    even, odd = k == 0, k == 1
    gp = lax.rem(g + 1, N_GZ)
    gm = lax.rem(g + N_GZ - 1, N_GZ)
    gp2 = lax.rem(g + 2, N_GZ)
    gm2 = lax.rem(g + N_GZ - 2, N_GZ)

    def remote(src, dst, ss, rs, cc, gg):
        return pltpu.make_async_remote_copy(
            src_ref=src, dst_ref=dst, send_sem=ss, recv_sem=rs, device_id=(cc, gg), device_id_type=MESH
        )

    def rows(i):
        return pl.ds(pl.multiple_of(i * XR, XR), XR)

    def own(i):
        return pltpu.make_async_copy(v_hbm.at[:, :, rows(i)], raw.at[i, :, pl.ds(3, 2)], own_s.at[i])

    def up(i):
        return remote(v_hbm.at[:, :, rows(i)], raw.at[i, :, pl.ds(1, 2)], up_s.at[i], up_r.at[i], c, gp)

    def down(i):
        return remote(v_hbm.at[:, :, rows(i)], raw.at[i, :, pl.ds(5, 2)], dn_s.at[i], dn_r.at[i], c, gm)

    def far(i):
        return remote(v_hbm.at[:, pl.ds(1, 1), rows(i)], raw.at[i, :, pl.ds(0, 1)], far_s.at[i], far_r.at[i], c, gp2)

    def forward(i):
        return remote(raw.at[i, :, pl.ds(2, 1)], raw.at[i, :, pl.ds(0, 1)], fwd_s.at[i], far_r.at[i], c, gp)

    def sites(i):
        return pl.ds(1 + i * XR, XR)

    def y_direct(i, lo, n, cc):
        return remote(
            u.at[pl.ds(lo, n), sites(i), pl.ds(0, K)], u.at[pl.ds(lo, n), sites(i), pl.ds(K, K)],
            y_s.at[i], y_r.at[i], cc, g,
        )

    def y_relay(i, lo, n, cc):
        return remote(
            u.at[pl.ds(lo, n), sites(i), pl.ds(0, K)], relay.at[i // 4, pl.ds(lo, n)],
            y_s.at[i], rel_r.at[i // 4], cc, g,
        )

    def relay_on(i, lo, n):
        return remote(
            relay.at[i // 4, pl.ds(lo, n)], u.at[pl.ds(lo, n), sites(i), pl.ds(K, K)],
            rel_s.at[i // 4], y_r.at[i], 3, g,
        )

    def g_forward(i):
        return remote(
            u.at[pl.ds(2, 1), sites(i), pl.ds(K, K)], u.at[pl.ds(0, 1), sites(i), pl.ds(K, K)],
            gf_s.at[i], gf_r.at[i], c, gp,
        )

    def out(i):
        return pltpu.make_async_copy(u.at[pl.ds(1, 2), sites(i)], u_hbm.at[:, rows(i)], out_s.at[i])

    def by_core(act):
        pl.when(even)(lambda: act(0, 3))
        pl.when(odd)(lambda: act(1, 2))

    @pl.loop(0, NC)
    def _(i):
        own(i).start()

    own_on = pltpu.make_async_copy(on_hbm, ons.at[pl.ds(2, 2), pl.ds(8, LX)], on_s.at[0])
    own_on.start()

    barrier = pltpu.get_barrier_semaphore()

    def greet(cc, gg):
        pl.semaphore_signal(barrier, inc=1, device_id=(cc, gg), device_id_type=MESH)

    greet(c, gp)
    greet(c, gm)

    @pl.when(even)
    def _():
        greet(c, gp2)
        greet(c, gm2)

    @pl.when(c > 0)
    def _():
        greet(c - 1, g)

    @pl.when(c < N_CUTS - 1)
    def _():
        greet(c + 1, g)

    @pl.when(c == 4)
    def _():
        greet(6, g)
        greet(7, g)

    @pl.when(c >= 6)
    def _():
        greet(4, g)

    @pl.when(c >= 5)
    def _():
        greet(3, g)

    @pl.when(c == 3)
    def _():
        greet(5, g)
        greet(6, g)
        greet(7, g)

    vt[:, pl.ds(0, 2)] = jnp.zeros((7, 2, K, LY), F32)
    vt[:, pl.ds(LX + 2, 2)] = jnp.zeros((7, 2, K, LY), F32)
    u[:, pl.ds(0, 1)] = jnp.zeros((3, 1, 2 * K, LY), F32)
    u[:, pl.ds(LX + 1, 1)] = jnp.zeros((3, 1, 2 * K, LY), F32)
    ons[:, pl.ds(0, 8)] = jnp.zeros((5, 8, LY), F32)
    ons[:, pl.ds(8 + LX, 8)] = jnp.zeros((5, 8, LY), F32)
    acc[...] = jnp.zeros_like(acc)

    @pl.when(c == N_CUTS - 1)
    def _():
        @pl.loop(0, LX)
        def _(x):
            for z in range(3):
                u[z, 1 + x, pl.ds(K, K)] = jnp.zeros((K, LY), F32)

    def one(p):
        return jnp.where(p, 1, 0)

    partners = 2 + 2 * one(even) + one(c > 0) + one(c < N_CUTS - 1) + one(c >= 6) + one(c >= 5)
    pl.semaphore_wait(barrier, partners + 2 * one(c == 4) + 3 * one(c == 3))

    on_up = remote(on_hbm, ons.at[pl.ds(0, 2), pl.ds(8, LX)], on_s.at[1], on_r.at[0], c, gp)
    on_dn = remote(on_hbm.at[pl.ds(0, 1)], ons.at[pl.ds(4, 1), pl.ds(8, LX)], on_s.at[2], on_r.at[1], c, gm)
    on_up.start()
    on_dn.start()

    @pl.loop(0, NC)
    def _(i):
        up(i).start()
        down(i).start()
        pl.when(even)(lambda: far(i).start())

    ctr, ih, c0, c1, c2 = (par[j] for j in range(5))

    def arrive(i):
        own(i).wait()
        up(i).wait_recv()
        pl.when(even)(lambda: forward(i).start())
        down(i).wait_recv()
        far(i).wait_recv()

        @pl.loop(0, 7)
        def _(z):
            vt[z, pl.ds(2 + i * XR, XR)] = jnp.swapaxes(raw[i, :, z], 0, 1)

    def apply_filter(i):
        @pl.loop(0, XR + 2)
        def _(r):
            x = i * XR - 1 + r
            for z in range(1, 6):
                v = vt[z, 2 + x]
                d = jnp.broadcast_to(ons[z - 1, pl.ds(8 + x, 1), :], (K, LY))
                around = vt[z - 1, 2 + x] + vt[z + 1, 2 + x] + vt[z, 1 + x] + vt[z, 3 + x] + lanes(v)
                first[z - 1, r] = ih * ((d - ctr) * v - around)

        @pl.when(i == 0)
        def _():
            first[:, pl.ds(0, 1)] = jnp.zeros((5, 1, K, LY), F32)

        @pl.when(i == NC - 1)
        def _():
            first[:, pl.ds(XR + 1, 1)] = jnp.zeros((5, 1, K, LY), F32)

        @pl.loop(0, XR)
        def _(r):
            x = i * XR + r
            for z in range(3):
                v = vt[z + 2, 2 + x]
                f = first[z + 1, r + 1]
                d = jnp.broadcast_to(ons[z + 1, pl.ds(8 + x, 1), :], (K, LY))
                around = first[z, r + 1] + first[z + 2, r + 1] + first[z + 1, r] + first[z + 1, r + 2] + lanes(f)
                second = 2.0 * (ih * ((d - ctr) * f - around)) - v
                u[z, 1 + x, pl.ds(0, K)] = c0 * v + c1 * f + c2 * second

    def send(i):
        row = lax.rem(i, 4)
        pl.when((c > 0) & (c != 4))(lambda: by_core(lambda lo, n: y_direct(i, lo, n, c - 1).start()))
        pl.when((c == 4) & (row == 0))(lambda: by_core(lambda lo, n: y_direct(i, lo, n, 3).start()))
        pl.when((c == 4) & (row != 0))(lambda: by_core(lambda lo, n: y_relay(i, lo, n, 4 + row).start()))

    def pass_on(i):
        row = lax.rem(i, 4)

        @pl.when((row != 0) & (c == 4 + row))
        def _():
            def act(lo, n):
                y_relay(i, lo, n, 4 + row).wait_recv()
                relay_on(i, lo, n).start()

            by_core(act)

    def g_arrive(i):
        @pl.when(c < N_CUTS - 1)
        def _():
            by_core(lambda lo, n: y_direct(i, lo, n, c).wait_recv())
            pl.when(even)(lambda: g_forward(i).start())
            pl.when(odd)(lambda: g_forward(i).wait_recv())

    def project(i):
        @pl.loop(0, XR)
        def _(r):
            x = i * XR + r
            for z in range(2):
                at = pl.ds(pl.multiple_of((z * XR + r) * LY, LY), LY)
                mid = u[z + 1, 1 + x]
                d = jnp.broadcast_to(ons[z + 2, pl.ds(8 + x, 1), :], (2 * K, LY))
                w = d * mid - (u[z + 1, x] + u[z + 1, 2 + x] + lanes(mid))
                if z == 0:
                    w = w - 2.0 * (u[0, 1 + x] + u[2, 1 + x])
                hi = mid.astype(BF16)
                w_hi = w.astype(BF16)
                ops[pl.ds(0, 64), at] = hi
                ops[pl.ds(64, 64), at] = (mid - hi.astype(F32)).astype(BF16)
                ops[pl.ds(128, 64), at] = w_hi
                ops[pl.ds(192, 64), at] = (w - w_hi.astype(F32)).astype(BF16)

        acc[...] += lax.dot_general(
            ops[pl.ds(0, 128)], ops[...], (((1,), (1,)), ((), ())), preferred_element_type=F32
        )
        out(i).start()

    own_on.wait()
    on_up.wait()
    on_dn.wait()
    arrive(0)

    @pl.loop(0, NC + LAG + 1)
    def _(i):
        @pl.when(i + 1 < NC)
        def _():
            arrive(i + 1)

        @pl.when(i < NC)
        def _():
            apply_filter(i)
            send(i)

        @pl.when((i >= 1) & (i <= NC))
        def _():
            pass_on(i - 1)

        @pl.when((i >= LAG) & (i < NC + LAG))
        def _():
            g_arrive(i - LAG)

        @pl.when(i >= LAG + 1)
        def _():
            project(i - LAG - 1)

    a = acc[...]
    acc_ref[:, pl.ds(0, 64)] = (a[0:64, 0:64] + a[64:128, 64:128]) + (a[0:64, 64:128] + a[64:128, 0:64])
    acc_ref[:, pl.ds(64, 64)] = (a[0:64, 128:192] + a[64:128, 192:256]) + (a[0:64, 192:256] + a[64:128, 128:192])

    @pl.loop(0, NC)
    def _(i):
        up(i).wait_send()
        down(i).wait_send()

        @pl.when(even)
        def _():
            far(i).wait_send()
            forward(i).wait_send()
            pl.when(c < N_CUTS - 1)(lambda: g_forward(i).wait_send())

        pl.when(c > 0)(lambda: by_core(lambda lo, n: y_direct(i, lo, n, c).wait_send()))
        row = lax.rem(i, 4)
        pl.when((row != 0) & (c == 4 + row))(lambda: by_core(lambda lo, n: relay_on(i, lo, n).wait_send()))
        out(i).wait()


def run_filter(v, onsite, params):
    dma = pltpu.SemaphoreType.DMA
    anyspace = pl.BlockSpec(memory_space=pl.ANY)
    return pl.pallas_call(
        filter_kernel,
        out_shape=(jax.ShapeDtypeStruct((2, LX, 2 * K, LY), F32), jax.ShapeDtypeStruct((2 * K, 128), F32)),
        in_specs=[anyspace, anyspace, pl.BlockSpec(memory_space=pltpu.SMEM)],
        out_specs=(anyspace, pl.BlockSpec(memory_space=pltpu.VMEM)),
        scratch_shapes=[
            pltpu.VMEM((NC, K, 7, XR, LY), F32),
            pltpu.VMEM((7, LX + 4, K, LY), F32),
            pltpu.VMEM((5, XR + 2, K, LY), F32),
            pltpu.VMEM((3, LX + 2, 2 * K, LY), F32),
            pltpu.VMEM((256, 2 * XR * LY), BF16),
            pltpu.VMEM((128, 256), F32),
            pltpu.VMEM((5, LX + 16, LY), F32),
            pltpu.VMEM((NC // 4, 3, XR, K, LY), F32),
            dma((NC,)), dma((3,)), dma((2,)),
            dma((NC,)), dma((NC,)), dma((NC,)), dma((NC,)), dma((NC,)), dma((NC,)), dma((NC,)),
            dma((NC,)), dma((NC,)), dma((NC // 4,)), dma((NC // 4,)), dma((NC,)), dma((NC,)), dma((NC,)),
        ],
        compiler_params=pltpu.CompilerParams(
            collective_id=0, has_side_effects=True, vmem_limit_bytes=60 << 20
        ),
        name="filter",
    )(v, onsite, params)


def solve_kernel(part_ref, linv_ref, proj_ref, half, got, zbuf, full, other, core_s, core_r, x_s, x_r, z_s, z_r, b_s, b_r):
    c = lax.axis_index("cuts")
    g = lax.axis_index("gz")
    k = lax.rem(g, 2)
    hi = lax.rem(g // 2, 2)
    z = g // 4
    mate = g + 1 - 2 * k
    across = g + 2 - 4 * hi

    def remote(src, dst, ss, rs, gg):
        return pltpu.make_async_remote_copy(
            src_ref=src, dst_ref=dst, send_sem=ss, recv_sem=rs, device_id=(c, gg), device_id_type=MESH
        )

    barrier = pltpu.get_barrier_semaphore()
    peers = [lax.rem(g + 4 * n, N_GZ) for n in range(1, 8)]
    for gg in [mate, across] + peers:
        pl.semaphore_signal(barrier, inc=1, device_id=(c, gg), device_id_type=MESH)
    pl.semaphore_wait(barrier, 9)

    mine = pl.ds(pl.multiple_of(32 * k, 32), 32)
    theirs = pl.ds(pl.multiple_of(32 - 32 * k, 32), 32)
    step = remote(part_ref.at[theirs], got.at[0], core_s, core_r, mate)
    step.start()
    step.wait()
    half[0] = part_ref[mine] + got[0]
    step = remote(half.at[0], got.at[1], x_s, x_r, across)
    step.start()
    step.wait()
    total = half[0] + got[1]
    half[1] = total
    zbuf[z] = total
    sends = [remote(half.at[1], zbuf.at[z], z_s.at[n - 1], z_r.at[n - 1], peers[n - 1]) for n in range(1, 8)]
    for s in sends:
        s.start()
    for n in range(1, 8):
        remote(half.at[1], zbuf.at[lax.rem(z - n + 8, 8)], z_s.at[n - 1], z_r.at[n - 1], peers[n - 1]).wait_recv()
    for s in sends:
        s.wait_send()
    t = [zbuf[n] for n in range(8)]
    full[mine] = ((t[0] + t[1]) + (t[2] + t[3])) + ((t[4] + t[5]) + (t[6] + t[7]))
    step = remote(full.at[mine], full.at[mine], b_s, b_r, mate)
    step.start()
    remote(full.at[theirs], full.at[theirs], b_s, b_r, mate).wait_recv()
    step.wait_send()

    both = full[...] * (1.0 / SITES)
    sub = lax.broadcasted_iota(jnp.int32, (64, 128), 0)
    lane = lax.broadcasted_iota(jnp.int32, (64, 128), 1)
    m = both[:, 64:128]
    a = jnp.where(lane < 64, both, 0.0) + jnp.where(lane == sub, 0.25, 0.0) + jnp.where(lane == sub + 64, 1.0, 0.0)
    for i in range(63):
        row = a[i : i + 1, :]
        scaled = row / row[:, i : i + 1]
        lo = (i + 1) // 8 * 8
        low = a[lo:, :]
        col = jnp.where(sub[lo:, :] > i, jnp.broadcast_to(low[:, i : i + 1], low.shape), 0.0)
        low = low - col * scaled
        a = low if lo == 0 else jnp.concatenate([a[:lo, :], low], 0)
    diag = jnp.sum(jnp.where(lane == sub, a, 0.0), axis=1, keepdims=True)
    linv = a[:, 64:128] * (1.0 / jnp.sqrt(diag))
    linv_ref[...] = linv

    def exact(p, q, dims):
        return lax.dot_general(p, q, (dims, ((), ())), precision=lax.Precision.HIGHEST, preferred_element_type=F32)

    right = exact(m, linv, ((1,), (1,)))
    p = exact(linv, right, ((1,), (0,)))
    proj_ref[0] = 0.5 * (p + p.T)


def run_solve(part):
    dma = pltpu.SemaphoreType.DMA
    vm = pl.BlockSpec(memory_space=pltpu.VMEM)
    return pl.pallas_call(
        solve_kernel,
        out_shape=(jax.ShapeDtypeStruct((64, 64), F32), jax.ShapeDtypeStruct((1, 64, 64), F32)),
        in_specs=[vm],
        out_specs=(vm, vm),
        scratch_shapes=[
            pltpu.VMEM((2, 32, 128), F32), pltpu.VMEM((2, 32, 128), F32), pltpu.VMEM((8, 32, 128), F32),
            pltpu.VMEM((64, 128), F32), pltpu.VMEM((64, 128), F32),
            dma, dma, dma, dma, dma((7,)), dma((7,)), dma, dma,
        ],
        compiler_params=pltpu.CompilerParams(collective_id=1, has_side_effects=True),
        name="solve",
    )(part)


XB = 16


def basis_kernel(linv_ref, u_ref, out_ref, tmp):
    linv = linv_ref[...]
    hi = linv.astype(BF16)
    lo = (linv - hi.astype(F32)).astype(BF16)
    left = jnp.concatenate([hi, lo, hi], 1)
    for x in range(0, XB, 2):
        right = []
        for s in range(2):
            t = u_ref[0, x + s]
            t_hi = t.astype(BF16)
            t_lo = (t - t_hi.astype(F32)).astype(BF16)
            right.append(jnp.concatenate([t_hi, t_hi, t_lo], 0))
        got = jnp.dot(left, jnp.concatenate(right, 1), preferred_element_type=F32)
        tmp[x] = got[:, :LY]
        tmp[x + 1] = got[:, LY:]
    for x in range(0, XB, 8):
        out_ref[0, :, 0, pl.ds(x, 8)] = jnp.swapaxes(tmp[pl.ds(x, 8)], 0, 1)


def run_basis(linv, u):
    return pl.pallas_call(
        basis_kernel,
        out_shape=jax.ShapeDtypeStruct((1, 2 * K, 2, LX, LY), F32),
        grid=(2, LX // XB),
        in_specs=[
            pl.BlockSpec((64, 64), lambda z, x: (0, 0)),
            pl.BlockSpec((1, XB, 2 * K, LY), lambda z, x: (z, x, 0, 0)),
        ],
        out_specs=pl.BlockSpec((1, 2 * K, 1, XB, LY), lambda z, x: (0, 0, z, x, 0)),
        scratch_shapes=[pltpu.VMEM((XB, 2 * K, LY), F32)],
        compiler_params=pltpu.CompilerParams(vmem_limit_bytes=32 << 20),
        name="basis",
    )(linv, u)


def body(vectors, onsite, center, inv_half, cheb_coef):
    params = jnp.concatenate([center, inv_half, cheb_coef[0]])
    u, part = run_filter(vectors[0], onsite, params)
    linv, projected = run_solve(part)
    return run_basis(linv, u), projected


def solution(mesh):
    in_specs = (
        P("cuts", None, "gz", None, None),
        P("gz", None, None),
        P("cuts"),
        P("cuts"),
        P("cuts", None),
    )
    out_specs = (P("cuts", None, "gz", None, None), P("cuts", None, None))
    return jax.shard_map(body, mesh=mesh, in_specs=in_specs, out_specs=out_specs, check_vma=False)
```

time: 659 us -> 288 us (0.44)
  the two profiles are of different devices: /device:TPU:24 before, /device:TPU:9 now
where the time goes in v1:
time: 288 us
  Pallas kernels  280 us (97%)
  local copies, waits for them, and re-layouts  4.75 us (2%)
    pallas_call x1, Pallas kernels, run_filter(): pl.pallas_call(filter_kernel, out_shape=(jax.ShapeDtypeStruct((2, LX, 2 *...  212 us
    pallas_call x1, Pallas kernels, run_solve(): pl.pallas_call(solve_kernel, out_shape=(jax.ShapeDtypeStruct((64, 64), F3...  59.3 us
    pallas_call x1, Pallas kernels, run_basis(): pl.pallas_call(basis_kernel, out_shape=jax.ShapeDtypeStruct((1, 2 * K, 2,...  9.28 us

profile of v1, /device:TPU:9, one launch (start us, length us, event | category | flops | bytes accessed | tf_op | source)
XLA Modules:
  0.0 288.2 jit_solution(1221802799383508845)
XLA Ops:
  1.9 1.2 pad_maximum_fusion.par
  3.2 211.7 %filter.1 = (f32[2,128,64,128]{3,2,1,0:T(8,128)}, f32[64,128]{1,0:T(8,128)}) custom-call(f32[32,2,128,128]{3,2,1,0:T(8,128)} %bitcast.2, f32[2,128,128]{2,1,0:T(8,128)} %on_hbm.1, f32[5]{0:T(128)} %pad_maximum_fusion.par), custom_call_target="tpu_custom_call" | custom-call | tf_op jit(solution)/shard_map/filter/pallas_call | solution.py:323
  214.8 59.3 %solve.1 = (f32[64,64]{1,0:T(8,128)}, f32[1,64,64]{2,1,0:T(8,128)}) custom-call(f32[64,128]{1,0:T(8,128)} %get-tuple-element.6.part_ref), custom_call_target="tpu_custom_call" | custom-call | tf_op jit(solution)/shard_map/solve/pallas_call | solution.py:422
  274.1 0.0 copy-start
  274.1 3.4 %copy-done = f32[2,128,64,128]{3,2,1,0:T(8,128)S(1)} copy-done((f32[2,128,64,128]{3,2,1,0:T(8,128)S(1)}, f32[2,128,64,128]{3,2,1,0:T(8,128)}, u32[]{:S(2)}) %copy-start) | copy-done | bytes 8388632
  277.5 0.0 copy-start.1
  277.5 0.8 copy-done.1
  278.3 0.0 copy-start.2
  278.3 9.3 %basis.1 = f32[1,64,2,128,128]{4,3,2,1,0:T(8,128)} custom-call(f32[64,64]{1,0:T(8,128)S(1)} %copy-done.1, f32[2,128,64,128]{3,2,1,0:T(8,128)S(1)} %copy-done), custom_call_target="tpu_custom_call" | custom-call | tf_op jit(solution)/shard_map/basis/pallas_call | solution.py:460
  287.5 0.0 copy-done.2
  287.5 0.6 copy.10
Async XLA Ops:
  274.1 3.4 %copy-start = (f32[2,128,64,128]{3,2,1,0:T(8,128)S(1)}, f32[2,128,64,128]{3,2,1,0:T(8,128)}, u32[]{:S(2)}) copy-start(f32[2,128,64,128]{3,2,1,0:T(8,128)} %get-tuple-element.8.u_ref) | copy-start | bytes 25165828
  277.5 0.8 copy-start.1
  278.3 9.3 %copy-start.2 = (f32[1,64,64]{2,1,0:T(8,128)S(1)}, f32[1,64,64]{2,1,0:T(8,128)}, u32[]{:S(2)}) copy-start(f32[1,64,64]{2,1,0:T(8,128)} %get-tuple-element.13) | copy-start | bytes 49156

commit v2 on v1

--- a/solution.py
+++ b/solution.py
@@ -13,7 +13,9 @@
 LY = 128
 XR = 8
 NC = LX // XR
-LAG = 2
+LAG = 3
+LAG_FAR = 6
+AHEAD = 3
 N_CUTS = 8
 N_GZ = 32
 SITES = 64 * 128 * 128
@@ -29,8 +31,8 @@
 
 
 def filter_kernel(
-    v_hbm, on_hbm, par, u_hbm, acc_ref,
-    raw, vt, first, u, ops, acc, ons, relay,
+    v_hbm, on_hbm, ctr_ref, ih_ref, cheb, f_hbm, g_hbm, acc_ref,
+    mine, below, above, far_in, vt, first, fs, gs, ops, acc, ons, relay,
     own_s, on_s, on_r, up_s, up_r, dn_s, dn_r, far_s, far_r, fwd_s, y_s, y_r,
     rel_s, rel_r, gf_s, gf_r, out_s,
 ):
@@ -51,50 +53,51 @@
     def rows(i):
         return pl.ds(pl.multiple_of(i * XR, XR), XR)
 
-    def own(i):
-        return pltpu.make_async_copy(v_hbm.at[:, :, rows(i)], raw.at[i, :, pl.ds(3, 2)], own_s.at[i])
+    def own(i, z):
+        return pltpu.make_async_copy(v_hbm.at[:, z, rows(i)], mine.at[i, z], own_s.at[z, i])
 
     def up(i):
-        return remote(v_hbm.at[:, :, rows(i)], raw.at[i, :, pl.ds(1, 2)], up_s.at[i], up_r.at[i], c, gp)
+        return remote(mine.at[i], below.at[i], up_s.at[i], up_r.at[i], c, gp)
 
     def down(i):
-        return remote(v_hbm.at[:, :, rows(i)], raw.at[i, :, pl.ds(5, 2)], dn_s.at[i], dn_r.at[i], c, gm)
+        return remote(mine.at[i], above.at[i], dn_s.at[i], dn_r.at[i], c, gm)
 
     def far(i):
-        return remote(v_hbm.at[:, pl.ds(1, 1), rows(i)], raw.at[i, :, pl.ds(0, 1)], far_s.at[i], far_r.at[i], c, gp2)
+        return remote(mine.at[i, 1], far_in.at[i], far_s.at[i], far_r.at[i], c, gp2)
 
     def forward(i):
-        return remote(raw.at[i, :, pl.ds(2, 1)], raw.at[i, :, pl.ds(0, 1)], fwd_s.at[i], far_r.at[i], c, gp)
-
-    def sites(i):
-        return pl.ds(1 + i * XR, XR)
+        return remote(below.at[i, 1], far_in.at[i], fwd_s.at[i], far_r.at[i], c, gp)
 
     def y_direct(i, lo, n, cc):
+        return remote(fs.at[1 + i, pl.ds(lo, n)], gs.at[1 + i, pl.ds(lo, n)], y_s.at[i], y_r.at[i], cc, g)
+
+    def y_relay(i, lo, n, cc):
+        return remote(fs.at[1 + i, pl.ds(lo, n)], relay.at[i // 4, pl.ds(lo, n)], y_s.at[i], rel_r.at[i // 4], cc, g)
+
+    def relay_on(i, lo, n):
+        return remote(relay.at[i // 4, pl.ds(lo, n)], gs.at[1 + i, pl.ds(lo, n)], rel_s.at[i // 4], y_r.at[i], 3, g)
+
+    def relay_twice(i, lo, n):
         return remote(
-            u.at[pl.ds(lo, n), sites(i), pl.ds(0, K)], u.at[pl.ds(lo, n), sites(i), pl.ds(K, K)],
-            y_s.at[i], y_r.at[i], cc, g,
+            relay.at[i // 4, pl.ds(lo, n)], relay.at[i // 4, pl.ds(lo, n)], rel_s.at[i // 4], rel_r.at[i // 4], 2, g
         )
 
-    def y_relay(i, lo, n, cc):
-        return remote(
-            u.at[pl.ds(lo, n), sites(i), pl.ds(0, K)], relay.at[i // 4, pl.ds(lo, n)],
-            y_s.at[i], rel_r.at[i // 4], cc, g,
-        )
-
-    def relay_on(i, lo, n):
-        return remote(
-            relay.at[i // 4, pl.ds(lo, n)], u.at[pl.ds(lo, n), sites(i), pl.ds(K, K)],
-            rel_s.at[i // 4], y_r.at[i], 3, g,
-        )
-
     def g_forward(i):
-        return remote(
-            u.at[pl.ds(2, 1), sites(i), pl.ds(K, K)], u.at[pl.ds(0, 1), sites(i), pl.ds(K, K)],
-            gf_s.at[i], gf_r.at[i], c, gp,
-        )
-
-    def out(i):
-        return pltpu.make_async_copy(u.at[pl.ds(1, 2), sites(i)], u_hbm.at[:, rows(i)], out_s.at[i])
+        return remote(gs.at[1 + i, 2], gs.at[1 + i, 0], gf_s.at[i], gf_r.at[i], c, gp)
+
+    def out_f(i):
+        return pltpu.make_async_copy(fs.at[1 + i, pl.ds(1, 2)], f_hbm.at[i], out_s.at[0, i])
+
+    def out_g(i):
+        return pltpu.make_async_copy(gs.at[1 + i, pl.ds(1, 2)], g_hbm.at[i], out_s.at[1, i])
+
+    def row_of(i):
+        m = lax.rem(i, 4)
+        return jnp.where(m == 0, 1, jnp.where(m == 1, 3, jnp.where(m == 2, 2, 0)))
+
+    def row_of(i):
+        m = lax.rem(i, 4)
+        return jnp.where(m == 0, 1, jnp.where(m == 1, 3, jnp.where(m == 2, 2, 0)))
 
     def by_core(act):
         pl.when(even)(lambda: act(0, 3))
@@ -102,7 +105,8 @@
 
     @pl.loop(0, NC)
     def _(i):
-        own(i).start()
+        own(i, 0).start()
+        own(i, 1).start()
 
     own_on = pltpu.make_async_copy(on_hbm, ons.at[pl.ds(2, 2), pl.ds(8, LX)], on_s.at[0])
     own_on.start()
@@ -136,21 +140,21 @@
     @pl.when(c >= 6)
     def _():
         greet(4, g)
-
-    @pl.when(c >= 5)
-    def _():
         greet(3, g)
 
     @pl.when(c == 3)
     def _():
-        greet(5, g)
         greet(6, g)
         greet(7, g)
 
+    pl.when(c == 5)(lambda: greet(2, g))
+    pl.when(c == 2)(lambda: greet(5, g))
+
     vt[:, pl.ds(0, 2)] = jnp.zeros((7, 2, K, LY), F32)
     vt[:, pl.ds(LX + 2, 2)] = jnp.zeros((7, 2, K, LY), F32)
-    u[:, pl.ds(0, 1)] = jnp.zeros((3, 1, 2 * K, LY), F32)
-    u[:, pl.ds(LX + 1, 1)] = jnp.zeros((3, 1, 2 * K, LY), F32)
+    for edge in (fs, gs):
+        edge[0, :, 7] = jnp.zeros((3, K, LY), F32)
+        edge[NC + 1, :, 0] = jnp.zeros((3, K, LY), F32)
     ons[:, pl.ds(0, 8)] = jnp.zeros((5, 8, LY), F32)
     ons[:, pl.ds(8 + LX, 8)] = jnp.zeros((5, 8, LY), F32)
     acc[...] = jnp.zeros_like(acc)
@@ -160,37 +164,43 @@
         @pl.loop(0, LX)
         def _(x):
             for z in range(3):
-                u[z, 1 + x, pl.ds(K, K)] = jnp.zeros((K, LY), F32)
+                gs[1 + x // XR, z, lax.rem(x, XR)] = jnp.zeros((K, LY), F32)
 
     def one(p):
         return jnp.where(p, 1, 0)
 
-    partners = 2 + 2 * one(even) + one(c > 0) + one(c < N_CUTS - 1) + one(c >= 6) + one(c >= 5)
-    pl.semaphore_wait(barrier, partners + 2 * one(c == 4) + 3 * one(c == 3))
+    partners = 2 + 2 * one(even) + one(c > 0) + one(c < N_CUTS - 1) + one(c == 5) + one(c == 2)
+    pl.semaphore_wait(barrier, partners + 2 * (one(c >= 6) + one(c == 4) + one(c == 3)))
 
     on_up = remote(on_hbm, ons.at[pl.ds(0, 2), pl.ds(8, LX)], on_s.at[1], on_r.at[0], c, gp)
     on_dn = remote(on_hbm.at[pl.ds(0, 1)], ons.at[pl.ds(4, 1), pl.ds(8, LX)], on_s.at[2], on_r.at[1], c, gm)
     on_up.start()
     on_dn.start()
 
-    @pl.loop(0, NC)
-    def _(i):
+    def v_send(i):
+        own(i, 0).wait()
+        own(i, 1).wait()
         up(i).start()
         down(i).start()
         pl.when(even)(lambda: far(i).start())
 
-    ctr, ih, c0, c1, c2 = (par[j] for j in range(5))
+    pl.loop(0, AHEAD)(v_send)
+
+    ctr, ih, c0, c1, c2 = ctr_ref[0], ih_ref[0], cheb[0, 0], cheb[0, 1], cheb[0, 2]
 
     def arrive(i):
-        own(i).wait()
         up(i).wait_recv()
         pl.when(even)(lambda: forward(i).start())
         down(i).wait_recv()
         far(i).wait_recv()
-
-        @pl.loop(0, 7)
+        to = pl.ds(2 + i * XR, XR)
+        vt[0, to] = jnp.swapaxes(far_in[i], 0, 1)
+
+        @pl.loop(0, 2)
         def _(z):
-            vt[z, pl.ds(2 + i * XR, XR)] = jnp.swapaxes(raw[i, :, z], 0, 1)
+            vt[1 + z, to] = jnp.swapaxes(below[i, z], 0, 1)
+            vt[3 + z, to] = jnp.swapaxes(mine[i, z], 0, 1)
+            vt[5 + z, to] = jnp.swapaxes(above[i, z], 0, 1)
 
     def apply_filter(i):
         @pl.loop(0, XR + 2)
@@ -219,24 +229,30 @@
                 d = jnp.broadcast_to(ons[z + 1, pl.ds(8 + x, 1), :], (K, LY))
                 around = first[z, r + 1] + first[z + 2, r + 1] + first[z + 1, r] + first[z + 1, r + 2] + lanes(f)
                 second = 2.0 * (ih * ((d - ctr) * f - around)) - v
-                u[z, 1 + x, pl.ds(0, K)] = c0 * v + c1 * f + c2 * second
+                fs[1 + i, z, r] = c0 * v + c1 * f + c2 * second
 
     def send(i):
-        row = lax.rem(i, 4)
+        row = row_of(i)
         pl.when((c > 0) & (c != 4))(lambda: by_core(lambda lo, n: y_direct(i, lo, n, c - 1).start()))
         pl.when((c == 4) & (row == 0))(lambda: by_core(lambda lo, n: y_direct(i, lo, n, 3).start()))
         pl.when((c == 4) & (row != 0))(lambda: by_core(lambda lo, n: y_relay(i, lo, n, 4 + row).start()))
 
-    def pass_on(i):
-        row = lax.rem(i, 4)
-
-        @pl.when((row != 0) & (c == 4 + row))
+    def pass_on(i, onward, here):
+        @pl.when(here)
         def _():
             def act(lo, n):
-                y_relay(i, lo, n, 4 + row).wait_recv()
-                relay_on(i, lo, n).start()
+                y_relay(i, lo, n, c).wait_recv()
+                onward(i, lo, n).start()
 
             by_core(act)
+
+    def pass_ons(i):
+        row = row_of(i)
+        pass_on(i, relay_on, (row >= 2) & (c == 4 + row))
+        pass_on(i, relay_twice, (row == 1) & (c == 5))
+
+    def pass_last(i):
+        pass_on(i, relay_on, (row_of(i) == 1) & (c == 2))
 
     def g_arrive(i):
         @pl.when(c < N_CUTS - 1)
@@ -249,52 +265,65 @@
         @pl.loop(0, XR)
         def _(r):
             x = i * XR + r
+            before, after = x + XR - 1, x + XR + 1
             for z in range(2):
                 at = pl.ds(pl.multiple_of((z * XR + r) * LY, LY), LY)
-                mid = u[z + 1, 1 + x]
-                d = jnp.broadcast_to(ons[z + 2, pl.ds(8 + x, 1), :], (2 * K, LY))
-                w = d * mid - (u[z + 1, x] + u[z + 1, 2 + x] + lanes(mid))
-                if z == 0:
-                    w = w - 2.0 * (u[0, 1 + x] + u[2, 1 + x])
-                hi = mid.astype(BF16)
-                w_hi = w.astype(BF16)
-                ops[pl.ds(0, 64), at] = hi
-                ops[pl.ds(64, 64), at] = (mid - hi.astype(F32)).astype(BF16)
-                ops[pl.ds(128, 64), at] = w_hi
-                ops[pl.ds(192, 64), at] = (w - w_hi.astype(F32)).astype(BF16)
+                d = jnp.broadcast_to(ons[z + 2, pl.ds(8 + x, 1), :], (K, LY))
+                for part, field in enumerate((fs, gs)):
+                    mid = field[1 + i, z + 1, r]
+                    around = field[before // XR, z + 1, lax.rem(before, XR)] + field[after // XR, z + 1, lax.rem(after, XR)]
+                    w = d * mid - (around + lanes(mid))
+                    if z == 0:
+                        w = w - 2.0 * (field[1 + i, 0, r] + field[1 + i, 2, r])
+                    hi = mid.astype(BF16)
+                    w_hi = w.astype(BF16)
+                    ops[pl.ds(part * K, K), at] = hi
+                    ops[pl.ds(64 + part * K, K), at] = (mid - hi.astype(F32)).astype(BF16)
+                    ops[pl.ds(128 + part * K, K), at] = w_hi
+                    ops[pl.ds(192 + part * K, K), at] = (w - w_hi.astype(F32)).astype(BF16)
 
         acc[...] += lax.dot_general(
             ops[pl.ds(0, 128)], ops[...], (((1,), (1,)), ((), ())), preferred_element_type=F32
         )
-        out(i).start()
+        out_f(i).start()
+        out_g(i).start()
 
     own_on.wait()
     on_up.wait()
     on_dn.wait()
     arrive(0)
 
-    @pl.loop(0, NC + LAG + 1)
+    lag = jnp.where(c == 3, LAG_FAR, LAG)
+
+    @pl.loop(0, NC + LAG_FAR + 1)
     def _(i):
         @pl.when(i + 1 < NC)
         def _():
             arrive(i + 1)
-
-        @pl.when(i < NC)
-        def _():
-            apply_filter(i)
-            send(i)
+            pl.when(i + AHEAD < NC)(lambda: v_send(i + AHEAD))
+
+        @pl.when(i < NC - 1)
+        def _():
+            @pl.loop(i, jnp.where(i == NC - 2, NC, i + 1))
+            def _(j):
+                apply_filter(j)
+                send(j)
 
         @pl.when((i >= 1) & (i <= NC))
         def _():
-            pass_on(i - 1)
-
-        @pl.when((i >= LAG) & (i < NC + LAG))
-        def _():
-            g_arrive(i - LAG)
-
-        @pl.when(i >= LAG + 1)
-        def _():
-            project(i - LAG - 1)
+            pass_ons(i - 1)
+
+        @pl.when((i >= 2) & (i <= NC + 1))
+        def _():
+            pass_last(i - 2)
+
+        @pl.when((i >= lag) & (i < NC + lag))
+        def _():
+            g_arrive(i - lag)
+
+        @pl.when((i >= lag + 1) & (i < NC + lag + 1))
+        def _():
+            project(i - lag - 1)
 
     a = acc[...]
     acc_ref[:, pl.ds(0, 64)] = (a[0:64, 0:64] + a[64:128, 64:128]) + (a[0:64, 64:128] + a[64:128, 0:64])
@@ -312,37 +341,47 @@
             pl.when(c < N_CUTS - 1)(lambda: g_forward(i).wait_send())
 
         pl.when(c > 0)(lambda: by_core(lambda lo, n: y_direct(i, lo, n, c).wait_send()))
-        row = lax.rem(i, 4)
-        pl.when((row != 0) & (c == 4 + row))(lambda: by_core(lambda lo, n: relay_on(i, lo, n).wait_send()))
-        out(i).wait()
-
-
-def run_filter(v, onsite, params):
+        row = row_of(i)
+        passed = (row >= 1) & ((c == 4 + row) | ((c == 2) & (row == 1)))
+        pl.when(passed)(lambda: by_core(lambda lo, n: relay_on(i, lo, n).wait_send()))
+        out_f(i).wait()
+        out_g(i).wait()
+
+
+def run_filter(v, onsite, center, inv_half, cheb):
     dma = pltpu.SemaphoreType.DMA
     anyspace = pl.BlockSpec(memory_space=pl.ANY)
     return pl.pallas_call(
         filter_kernel,
-        out_shape=(jax.ShapeDtypeStruct((2, LX, 2 * K, LY), F32), jax.ShapeDtypeStruct((2 * K, 128), F32)),
-        in_specs=[anyspace, anyspace, pl.BlockSpec(memory_space=pltpu.SMEM)],
-        out_specs=(anyspace, pl.BlockSpec(memory_space=pltpu.VMEM)),
+        out_shape=(
+            jax.ShapeDtypeStruct((NC, 2, XR, K, LY), F32),
+            jax.ShapeDtypeStruct((NC, 2, XR, K, LY), F32),
+            jax.ShapeDtypeStruct((2 * K, 128), F32),
+        ),
+        in_specs=[anyspace, anyspace] + [pl.BlockSpec(memory_space=pltpu.SMEM)] * 3,
+        out_specs=(anyspace, anyspace, pl.BlockSpec(memory_space=pltpu.VMEM)),
         scratch_shapes=[
-            pltpu.VMEM((NC, K, 7, XR, LY), F32),
+            pltpu.VMEM((NC, 2, K, XR, LY), F32),
+            pltpu.VMEM((NC, 2, K, XR, LY), F32),
+            pltpu.VMEM((NC, 2, K, XR, LY), F32),
+            pltpu.VMEM((NC, K, XR, LY), F32),
             pltpu.VMEM((7, LX + 4, K, LY), F32),
             pltpu.VMEM((5, XR + 2, K, LY), F32),
-            pltpu.VMEM((3, LX + 2, 2 * K, LY), F32),
+            pltpu.VMEM((NC + 2, 3, XR, K, LY), F32),
+            pltpu.VMEM((NC + 2, 3, XR, K, LY), F32),
             pltpu.VMEM((256, 2 * XR * LY), BF16),
             pltpu.VMEM((128, 256), F32),
             pltpu.VMEM((5, LX + 16, LY), F32),
             pltpu.VMEM((NC // 4, 3, XR, K, LY), F32),
-            dma((NC,)), dma((3,)), dma((2,)),
+            dma((2, NC)), dma((3,)), dma((2,)),
             dma((NC,)), dma((NC,)), dma((NC,)), dma((NC,)), dma((NC,)), dma((NC,)), dma((NC,)),
-            dma((NC,)), dma((NC,)), dma((NC // 4,)), dma((NC // 4,)), dma((NC,)), dma((NC,)), dma((NC,)),
+            dma((NC,)), dma((NC,)), dma((NC // 4,)), dma((NC // 4,)), dma((NC,)), dma((NC,)), dma((2, NC)),
         ],
         compiler_params=pltpu.CompilerParams(
             collective_id=0, has_side_effects=True, vmem_limit_bytes=60 << 20
         ),
         name="filter",
-    )(v, onsite, params)
+    )(v, onsite, center, inv_half, cheb)
 
 
 def solve_kernel(part_ref, linv_ref, proj_ref, half, got, zbuf, full, other, core_s, core_r, x_s, x_r, z_s, z_r, b_s, b_r):
@@ -434,49 +473,46 @@
     )(part)
 
 
-XB = 16
-
-
-def basis_kernel(linv_ref, u_ref, out_ref, tmp):
+def basis_kernel(linv_ref, p_ref, f_ref, g_ref, out_ref, proj_ref, tmp):
+    proj_ref[...] = p_ref[...]
     linv = linv_ref[...]
     hi = linv.astype(BF16)
     lo = (linv - hi.astype(F32)).astype(BF16)
     left = jnp.concatenate([hi, lo, hi], 1)
-    for x in range(0, XB, 2):
-        right = []
-        for s in range(2):
-            t = u_ref[0, x + s]
-            t_hi = t.astype(BF16)
-            t_lo = (t - t_hi.astype(F32)).astype(BF16)
-            right.append(jnp.concatenate([t_hi, t_hi, t_lo], 0))
-        got = jnp.dot(left, jnp.concatenate(right, 1), preferred_element_type=F32)
-        tmp[x] = got[:, :LY]
-        tmp[x + 1] = got[:, LY:]
-    for x in range(0, XB, 8):
-        out_ref[0, :, 0, pl.ds(x, 8)] = jnp.swapaxes(tmp[pl.ds(x, 8)], 0, 1)
-
-
-def run_basis(linv, u):
+    for n in range(2):
+        for z in range(2):
+            for x in range(0, XR, 2):
+                right = []
+                for s in range(2):
+                    t = jnp.concatenate([f_ref[n, z, x + s], g_ref[n, z, x + s]], 0)
+                    t_hi = t.astype(BF16)
+                    t_lo = (t - t_hi.astype(F32)).astype(BF16)
+                    right.append(jnp.concatenate([t_hi, t_hi, t_lo], 0))
+                got = jnp.dot(left, jnp.concatenate(right, 1), preferred_element_type=F32)
+                tmp[x] = got[:, :LY]
+                tmp[x + 1] = got[:, LY:]
+            out_ref[0, :, z, pl.ds(n * XR, XR)] = jnp.swapaxes(tmp[...], 0, 1)
+
+
+def run_basis(linv, p, f, g):
+    small = pl.BlockSpec((1, 64, 64), lambda i: (0, 0, 0))
+    half = pl.BlockSpec((2, 2, XR, K, LY), lambda i: (i, 0, 0, 0, 0))
     return pl.pallas_call(
         basis_kernel,
-        out_shape=jax.ShapeDtypeStruct((1, 2 * K, 2, LX, LY), F32),
-        grid=(2, LX // XB),
-        in_specs=[
-            pl.BlockSpec((64, 64), lambda z, x: (0, 0)),
-            pl.BlockSpec((1, XB, 2 * K, LY), lambda z, x: (z, x, 0, 0)),
-        ],
-        out_specs=pl.BlockSpec((1, 2 * K, 1, XB, LY), lambda z, x: (0, 0, z, x, 0)),
-        scratch_shapes=[pltpu.VMEM((XB, 2 * K, LY), F32)],
-        compiler_params=pltpu.CompilerParams(vmem_limit_bytes=32 << 20),
+        out_shape=(jax.ShapeDtypeStruct((1, 2 * K, 2, LX, LY), F32), jax.ShapeDtypeStruct((1, 64, 64), F32)),
+        grid=(NC // 2,),
+        in_specs=[pl.BlockSpec((64, 64), lambda i: (0, 0)), small, half, half],
+        out_specs=(pl.BlockSpec((1, 2 * K, 2, 2 * XR, LY), lambda i: (0, 0, 0, i, 0)), small),
+        scratch_shapes=[pltpu.VMEM((XR, 2 * K, LY), F32)],
+        compiler_params=pltpu.CompilerParams(vmem_limit_bytes=60 << 20),
         name="basis",
-    )(linv, u)
+    )(linv, p, f, g)
 
 
 def body(vectors, onsite, center, inv_half, cheb_coef):
-    params = jnp.concatenate([center, inv_half, cheb_coef[0]])
-    u, part = run_filter(vectors[0], onsite, params)
+    f, g, part = run_filter(vectors[0], onsite, center, inv_half, cheb_coef)
     linv, projected = run_solve(part)
-    return run_basis(linv, u), projected
+    return run_basis(linv, projected, f, g)
 
 
 def solution(mesh):

time: 288 us -> 225 us (0.78)
  Pallas kernels: 280 us -> 222 us
  local copies, waits for them, and re-layouts: 4.75 us -> 0 us
    pallas_call x1, Pallas kernels: 59.3 us -> 24.7 us  [run_solve(): pl.pallas_call(solve_kernel, out_shape=(jax.ShapeDtypeStruct((64, 64), F3...]
    pallas_call x2, Pallas kernels: 221 us -> 198 us  [the longest x1 187 us: run_filter(): pl.pallas_call(filter_kernel, out_shape=(jax.ShapeDtypeStruct((NC, 2, XR,...]
    unnamed x7 -> x0, local copies, waits for them, and re-layouts: 4.75 us -> none
where the time goes in v2:
time: 225 us; the launch traced here: 224 us
  Pallas kernels  222 us (99%)
    pallas_call x1, Pallas kernels, run_filter(): pl.pallas_call(filter_kernel, out_shape=(jax.ShapeDtypeStruct((NC, 2, XR,...  187 us
    pallas_call x1, Pallas kernels, run_solve(): pl.pallas_call(solve_kernel, out_shape=(jax.ShapeDtypeStruct((64, 64), F3...  24.7 us
    pallas_call x1, Pallas kernels, run_basis(): pl.pallas_call(basis_kernel, out_shape=(jax.ShapeDtypeStruct((1, 2 * K, 2...  10.7 us

profile of v2, /device:TPU:9, one launch (start us, length us, event | category | flops | bytes accessed | tf_op | source)
XLA Modules:
  0.0 224.2 jit_solution(18231675393484129062)
XLA Ops:
  1.9 186.8 %filter.1 = (f32[16,2,8,32,128]{4,3,2,1,0:T(8,128)}, f32[16,2,8,32,128]{4,3,2,1,0:T(8,128)}, f32[64,128]{1,0:T(8,128)}) custom-call(f32[32,2,128,128]{3,2,1,0:T(8,128)} %bitcast.1, f32[2,128,128]{2,1,0:T(8,128)} %on_hbm.1, f32[1]{0:T(128)S(6)} %copy.7.ctr_ref, f32[1]{0:T(128)S(6)} %copy.8.ih_ref, f32[1,3]{1,0:T(1,128)} %cheb.1), custom_call_target="tpu_custom_call" | custom-call | tf_op jit(solution)/shard_map/filter/pallas_call | solution.py:354
  188.8 24.7 %solve.1 = (f32[64,64]{1,0:T(8,128)}, f32[1,64,64]{2,1,0:T(8,128)}) custom-call(f32[64,128]{1,0:T(8,128)} %get-tuple-element.7.part_ref), custom_call_target="tpu_custom_call" | custom-call | tf_op jit(solution)/shard_map/solve/pallas_call | solution.py:461
  213.5 10.7 %basis.1 = (f32[1,64,2,128,128]{4,3,2,1,0:T(8,128)}, f32[1,64,64]{2,1,0:T(8,128)}) custom-call(f32[64,64]{1,0:T(8,128)} %get-tuple-element.8.linv_ref, f32[1,64,64]{2,1,0:T(8,128)} %get-tuple-element.9.p_ref, f32[16,2,8,32,128]{4,3,2,1,0:T(8,128)} %get-tuple-element.10.f_ref, f32[16,2,8,32,128]{4,3,2,1,0:T(8,128)} %get-tuple-element.11.g_ref), custom_call_target="tpu_custom_call" | custom-call | tf_op jit(solution)/shard_map/basis/pallas_call | solution.py:500

commit v3 on v2

--- a/solution.py
+++ b/solution.py
@@ -30,11 +30,69 @@
     return left + right
 
 
+def solve(c, g, remote, part, linv_ref, proj_ref, half, got, zbuf, full, core_s, core_r, x_s, x_r, z_s, z_r, b_s, b_r):
+    k = lax.rem(g, 2)
+    z = g // 4
+    mate = g + 1 - 2 * k
+    across = g + 2 - 4 * lax.rem(g // 2, 2)
+    peers = [lax.rem(g + 4 * n, N_GZ) for n in range(1, 8)]
+
+    my_rows = pl.ds(pl.multiple_of(32 * k, 32), 32)
+    theirs = pl.ds(pl.multiple_of(32 - 32 * k, 32), 32)
+    step = remote(part.at[theirs], got.at[0], core_s, core_r, c, mate)
+    step.start()
+    step.wait()
+    half[0] = part[my_rows] + got[0]
+    step = remote(half.at[0], got.at[1], x_s, x_r, c, across)
+    step.start()
+    step.wait()
+    total = half[0] + got[1]
+    half[1] = total
+    zbuf[z] = total
+    sends = [remote(half.at[1], zbuf.at[z], z_s.at[n - 1], z_r.at[n - 1], c, peers[n - 1]) for n in range(1, 8)]
+    for s in sends:
+        s.start()
+    for n in range(1, 8):
+        remote(half.at[1], zbuf.at[lax.rem(z - n + 8, 8)], z_s.at[n - 1], z_r.at[n - 1], c, peers[n - 1]).wait_recv()
+    for s in sends:
+        s.wait_send()
+    t = [zbuf[n] for n in range(8)]
+    full[my_rows] = ((t[0] + t[1]) + (t[2] + t[3])) + ((t[4] + t[5]) + (t[6] + t[7]))
+    step = remote(full.at[my_rows], full.at[my_rows], b_s, b_r, c, mate)
+    step.start()
+    remote(full.at[theirs], full.at[theirs], b_s, b_r, c, mate).wait_recv()
+    step.wait_send()
+
+    both = full[...] * (1.0 / SITES)
+    sub = lax.broadcasted_iota(jnp.int32, (64, 128), 0)
+    lane = lax.broadcasted_iota(jnp.int32, (64, 128), 1)
+    m = both[:, 64:128]
+    a = jnp.where(lane < 64, both, 0.0) + jnp.where(lane == sub, 0.25, 0.0) + jnp.where(lane == sub + 64, 1.0, 0.0)
+    for i in range(63):
+        row = a[i : i + 1, :]
+        scaled = row / row[:, i : i + 1]
+        lo = (i + 1) // 8 * 8
+        low = a[lo:, :]
+        col = jnp.where(sub[lo:, :] > i, jnp.broadcast_to(low[:, i : i + 1], low.shape), 0.0)
+        low = low - col * scaled
+        a = low if lo == 0 else jnp.concatenate([a[:lo, :], low], 0)
+    diag = jnp.sum(jnp.where(lane == sub, a, 0.0), axis=1, keepdims=True)
+    linv = a[:, 64:128] * (1.0 / jnp.sqrt(diag))
+    linv_ref[...] = linv
+
+    def exact(p, q, dims):
+        return lax.dot_general(p, q, (dims, ((), ())), precision=lax.Precision.HIGHEST, preferred_element_type=F32)
+
+    right = exact(m, linv, ((1,), (1,)))
+    p = exact(linv, right, ((1,), (0,)))
+    proj_ref[0] = 0.5 * (p + p.T)
+
+
 def filter_kernel(
-    v_hbm, on_hbm, ctr_ref, ih_ref, cheb, f_hbm, g_hbm, acc_ref,
+    v_hbm, on_hbm, ctr_ref, ih_ref, cheb, f_hbm, g_hbm, linv_ref, proj_ref,
     mine, below, above, far_in, vt, first, fs, gs, ops, acc, ons, relay,
     own_s, on_s, on_r, up_s, up_r, dn_s, dn_r, far_s, far_r, fwd_s, y_s, y_r,
-    rel_s, rel_r, gf_s, gf_r, out_s,
+    rel_s, rel_r, gf_s, gf_r, out_s, part, *solve_scratch,
 ):
     c = lax.axis_index("cuts")
     g = lax.axis_index("gz")
@@ -150,6 +208,10 @@
     pl.when(c == 5)(lambda: greet(2, g))
     pl.when(c == 2)(lambda: greet(5, g))
 
+    greet(c, g + 2 - 4 * lax.rem(g // 2, 2))
+    for n in range(1, 8):
+        greet(c, lax.rem(g + 4 * n, N_GZ))
+
     vt[:, pl.ds(0, 2)] = jnp.zeros((7, 2, K, LY), F32)
     vt[:, pl.ds(LX + 2, 2)] = jnp.zeros((7, 2, K, LY), F32)
     for edge in (fs, gs):
@@ -169,7 +231,7 @@
     def one(p):
         return jnp.where(p, 1, 0)
 
-    partners = 2 + 2 * one(even) + one(c > 0) + one(c < N_CUTS - 1) + one(c == 5) + one(c == 2)
+    partners = 10 + 2 * one(even) + one(c > 0) + one(c < N_CUTS - 1) + one(c == 5) + one(c == 2)
     pl.semaphore_wait(barrier, partners + 2 * (one(c >= 6) + one(c == 4) + one(c == 3)))
 
     on_up = remote(on_hbm, ons.at[pl.ds(0, 2), pl.ds(8, LX)], on_s.at[1], on_r.at[0], c, gp)
@@ -326,8 +388,9 @@
             project(i - lag - 1)
 
     a = acc[...]
-    acc_ref[:, pl.ds(0, 64)] = (a[0:64, 0:64] + a[64:128, 64:128]) + (a[0:64, 64:128] + a[64:128, 0:64])
-    acc_ref[:, pl.ds(64, 64)] = (a[0:64, 128:192] + a[64:128, 192:256]) + (a[0:64, 192:256] + a[64:128, 128:192])
+    part[:, pl.ds(0, 64)] = (a[0:64, 0:64] + a[64:128, 64:128]) + (a[0:64, 64:128] + a[64:128, 0:64])
+    part[:, pl.ds(64, 64)] = (a[0:64, 128:192] + a[64:128, 192:256]) + (a[0:64, 192:256] + a[64:128, 128:192])
+    solve(c, g, remote, part, linv_ref, proj_ref, *solve_scratch)
 
     @pl.loop(0, NC)
     def _(i):
@@ -356,10 +419,11 @@
         out_shape=(
             jax.ShapeDtypeStruct((NC, 2, XR, K, LY), F32),
             jax.ShapeDtypeStruct((NC, 2, XR, K, LY), F32),
-            jax.ShapeDtypeStruct((2 * K, 128), F32),
+            jax.ShapeDtypeStruct((64, 64), F32),
+            jax.ShapeDtypeStruct((1, 64, 64), F32),
         ),
         in_specs=[anyspace, anyspace] + [pl.BlockSpec(memory_space=pltpu.SMEM)] * 3,
-        out_specs=(anyspace, anyspace, pl.BlockSpec(memory_space=pltpu.VMEM)),
+        out_specs=(anyspace, anyspace, pl.BlockSpec(memory_space=pltpu.VMEM), pl.BlockSpec(memory_space=pltpu.VMEM)),
         scratch_shapes=[
             pltpu.VMEM((NC, 2, K, XR, LY), F32),
             pltpu.VMEM((NC, 2, K, XR, LY), F32),
@@ -376,6 +440,10 @@
             dma((2, NC)), dma((3,)), dma((2,)),
             dma((NC,)), dma((NC,)), dma((NC,)), dma((NC,)), dma((NC,)), dma((NC,)), dma((NC,)),
             dma((NC,)), dma((NC,)), dma((NC // 4,)), dma((NC // 4,)), dma((NC,)), dma((NC,)), dma((2, NC)),
+            pltpu.VMEM((64, 128), F32),
+            pltpu.VMEM((2, 32, 128), F32), pltpu.VMEM((2, 32, 128), F32), pltpu.VMEM((8, 32, 128), F32),
+            pltpu.VMEM((64, 128), F32),
+            dma, dma, dma, dma, dma((7,)), dma((7,)), dma, dma,
         ],
         compiler_params=pltpu.CompilerParams(
             collective_id=0, has_side_effects=True, vmem_limit_bytes=60 << 20
@@ -384,102 +452,13 @@
     )(v, onsite, center, inv_half, cheb)
 
 
-def solve_kernel(part_ref, linv_ref, proj_ref, half, got, zbuf, full, other, core_s, core_r, x_s, x_r, z_s, z_r, b_s, b_r):
-    c = lax.axis_index("cuts")
-    g = lax.axis_index("gz")
-    k = lax.rem(g, 2)
-    hi = lax.rem(g // 2, 2)
-    z = g // 4
-    mate = g + 1 - 2 * k
-    across = g + 2 - 4 * hi
-
-    def remote(src, dst, ss, rs, gg):
-        return pltpu.make_async_remote_copy(
-            src_ref=src, dst_ref=dst, send_sem=ss, recv_sem=rs, device_id=(c, gg), device_id_type=MESH
-        )
-
-    barrier = pltpu.get_barrier_semaphore()
-    peers = [lax.rem(g + 4 * n, N_GZ) for n in range(1, 8)]
-    for gg in [mate, across] + peers:
-        pl.semaphore_signal(barrier, inc=1, device_id=(c, gg), device_id_type=MESH)
-    pl.semaphore_wait(barrier, 9)
-
-    mine = pl.ds(pl.multiple_of(32 * k, 32), 32)
-    theirs = pl.ds(pl.multiple_of(32 - 32 * k, 32), 32)
-    step = remote(part_ref.at[theirs], got.at[0], core_s, core_r, mate)
-    step.start()
-    step.wait()
-    half[0] = part_ref[mine] + got[0]
-    step = remote(half.at[0], got.at[1], x_s, x_r, across)
-    step.start()
-    step.wait()
-    total = half[0] + got[1]
-    half[1] = total
-    zbuf[z] = total
-    sends = [remote(half.at[1], zbuf.at[z], z_s.at[n - 1], z_r.at[n - 1], peers[n - 1]) for n in range(1, 8)]
-    for s in sends:
-        s.start()
-    for n in range(1, 8):
-        remote(half.at[1], zbuf.at[lax.rem(z - n + 8, 8)], z_s.at[n - 1], z_r.at[n - 1], peers[n - 1]).wait_recv()
-    for s in sends:
-        s.wait_send()
-    t = [zbuf[n] for n in range(8)]
-    full[mine] = ((t[0] + t[1]) + (t[2] + t[3])) + ((t[4] + t[5]) + (t[6] + t[7]))
-    step = remote(full.at[mine], full.at[mine], b_s, b_r, mate)
-    step.start()
-    remote(full.at[theirs], full.at[theirs], b_s, b_r, mate).wait_recv()
-    step.wait_send()
-
-    both = full[...] * (1.0 / SITES)
-    sub = lax.broadcasted_iota(jnp.int32, (64, 128), 0)
-    lane = lax.broadcasted_iota(jnp.int32, (64, 128), 1)
-    m = both[:, 64:128]
-    a = jnp.where(lane < 64, both, 0.0) + jnp.where(lane == sub, 0.25, 0.0) + jnp.where(lane == sub + 64, 1.0, 0.0)
-    for i in range(63):
-        row = a[i : i + 1, :]
-        scaled = row / row[:, i : i + 1]
-        lo = (i + 1) // 8 * 8
-        low = a[lo:, :]
-        col = jnp.where(sub[lo:, :] > i, jnp.broadcast_to(low[:, i : i + 1], low.shape), 0.0)
-        low = low - col * scaled
-        a = low if lo == 0 else jnp.concatenate([a[:lo, :], low], 0)
-    diag = jnp.sum(jnp.where(lane == sub, a, 0.0), axis=1, keepdims=True)
-    linv = a[:, 64:128] * (1.0 / jnp.sqrt(diag))
-    linv_ref[...] = linv
-
-    def exact(p, q, dims):
-        return lax.dot_general(p, q, (dims, ((), ())), precision=lax.Precision.HIGHEST, preferred_element_type=F32)
-
-    right = exact(m, linv, ((1,), (1,)))
-    p = exact(linv, right, ((1,), (0,)))
-    proj_ref[0] = 0.5 * (p + p.T)
-
-
-def run_solve(part):
-    dma = pltpu.SemaphoreType.DMA
-    vm = pl.BlockSpec(memory_space=pltpu.VMEM)
-    return pl.pallas_call(
-        solve_kernel,
-        out_shape=(jax.ShapeDtypeStruct((64, 64), F32), jax.ShapeDtypeStruct((1, 64, 64), F32)),
-        in_specs=[vm],
-        out_specs=(vm, vm),
-        scratch_shapes=[
-            pltpu.VMEM((2, 32, 128), F32), pltpu.VMEM((2, 32, 128), F32), pltpu.VMEM((8, 32, 128), F32),
-            pltpu.VMEM((64, 128), F32), pltpu.VMEM((64, 128), F32),
-            dma, dma, dma, dma, dma((7,)), dma((7,)), dma, dma,
-        ],
-        compiler_params=pltpu.CompilerParams(collective_id=1, has_side_effects=True),
-        name="solve",
-    )(part)
-
-
 def basis_kernel(linv_ref, p_ref, f_ref, g_ref, out_ref, proj_ref, tmp):
     proj_ref[...] = p_ref[...]
     linv = linv_ref[...]
     hi = linv.astype(BF16)
     lo = (linv - hi.astype(F32)).astype(BF16)
     left = jnp.concatenate([hi, lo, hi], 1)
-    for n in range(2):
+    for n in range(4):
         for z in range(2):
             for x in range(0, XR, 2):
                 right = []
@@ -496,13 +475,13 @@
 
 def run_basis(linv, p, f, g):
     small = pl.BlockSpec((1, 64, 64), lambda i: (0, 0, 0))
-    half = pl.BlockSpec((2, 2, XR, K, LY), lambda i: (i, 0, 0, 0, 0))
+    half = pl.BlockSpec((4, 2, XR, K, LY), lambda i: (i, 0, 0, 0, 0))
     return pl.pallas_call(
         basis_kernel,
         out_shape=(jax.ShapeDtypeStruct((1, 2 * K, 2, LX, LY), F32), jax.ShapeDtypeStruct((1, 64, 64), F32)),
-        grid=(NC // 2,),
+        grid=(NC // 4,),
         in_specs=[pl.BlockSpec((64, 64), lambda i: (0, 0)), small, half, half],
-        out_specs=(pl.BlockSpec((1, 2 * K, 2, 2 * XR, LY), lambda i: (0, 0, 0, i, 0)), small),
+        out_specs=(pl.BlockSpec((1, 2 * K, 2, 4 * XR, LY), lambda i: (0, 0, 0, i, 0)), small),
         scratch_shapes=[pltpu.VMEM((XR, 2 * K, LY), F32)],
         compiler_params=pltpu.CompilerParams(vmem_limit_bytes=60 << 20),
         name="basis",
@@ -510,8 +489,7 @@
 
 
 def body(vectors, onsite, center, inv_half, cheb_coef):
-    f, g, part = run_filter(vectors[0], onsite, center, inv_half, cheb_coef)
-    linv, projected = run_solve(part)
+    f, g, linv, projected = run_filter(vectors[0], onsite, center, inv_half, cheb_coef)
     return run_basis(linv, projected, f, g)
 
 

time: 225 us -> 220 us (0.978)
  Pallas kernels: 222 us -> 218 us
    pallas_call x1 -> x0, Pallas kernels: 24.7 us -> none  [run_solve(): pl.pallas_call(solve_kernel, out_shape=(jax.ShapeDtypeStruct((64, 64), F3...]
    pallas_call x1, Pallas kernels: 187 us -> 209 us  [run_filter(): pl.pallas_call(filter_kernel, out_shape=(jax.ShapeDtypeStruct((NC, 2, XR,...]
where the time goes in v3:
time: 220 us
  Pallas kernels  218 us (99%)
    pallas_call x1, Pallas kernels, run_filter(): pl.pallas_call(filter_kernel, out_shape=(jax.ShapeDtypeStruct((NC, 2, XR,...  209 us
    pallas_call x1, Pallas kernels, run_basis(): pl.pallas_call(basis_kernel, out_shape=(jax.ShapeDtypeStruct((1, 2 * K, 2...  8.81 us

profile of v3, /device:TPU:9, one launch (start us, length us, event | category | flops | bytes accessed | tf_op | source)
XLA Modules:
  0.0 219.9 jit_solution(1343906310969516073)
XLA Ops:
  1.9 209.1 %filter.1 = (f32[16,2,8,32,128]{4,3,2,1,0:T(8,128)}, f32[16,2,8,32,128]{4,3,2,1,0:T(8,128)}, f32[64,64]{1,0:T(8,128)}, f32[1,64,64]{2,1,0:T(8,128)}) custom-call(f32[32,2,128,128]{3,2,1,0:T(8,128)} %bitcast.1, f32[2,128,128]{2,1,0:T(8,128)} %on_hbm.1, f32[1]{0:T(128)S(6)} %copy.7.ctr_ref, f32[1]{0:T(128)S(6)} %copy.8.ih_ref, f32[1,3]{1,0:T(1,128)} %cheb.1), custom_call_target="tpu_custom_call" | custom-call | tf_op jit(solution)/shard_map/filter/pallas_call | solution.py:417
  211.0 8.8 %basis.1 = (f32[1,64,2,128,128]{4,3,2,1,0:T(8,128)}, f32[1,64,64]{2,1,0:T(8,128)}) custom-call(f32[64,64]{1,0:T(8,128)} %get-tuple-element.6.linv_ref, f32[1,64,64]{2,1,0:T(8,128)} %get-tuple-element.7.p_ref, f32[16,2,8,32,128]{4,3,2,1,0:T(8,128)} %get-tuple-element.8.f_ref, f32[16,2,8,32,128]{4,3,2,1,0:T(8,128)} %get-tuple-element.9.g_ref), custom_call_target="tpu_custom_call" | custom-call | tf_op jit(solution)/shard_map/basis/pallas_call | solution.py:479

commit v4 on v3

--- a/solution.py
+++ b/solution.py
@@ -13,8 +13,8 @@
 LY = 128
 XR = 8
 NC = LX // XR
-LAG = 3
-LAG_FAR = 6
+LAG = 2
+LAG_FAR = 5
 AHEAD = 3
 N_CUTS = 8
 N_GZ = 32
@@ -458,7 +458,7 @@
     hi = linv.astype(BF16)
     lo = (linv - hi.astype(F32)).astype(BF16)
     left = jnp.concatenate([hi, lo, hi], 1)
-    for n in range(4):
+    for n in range(8):
         for z in range(2):
             for x in range(0, XR, 2):
                 right = []
@@ -475,13 +475,13 @@
 
 def run_basis(linv, p, f, g):
     small = pl.BlockSpec((1, 64, 64), lambda i: (0, 0, 0))
-    half = pl.BlockSpec((4, 2, XR, K, LY), lambda i: (i, 0, 0, 0, 0))
+    half = pl.BlockSpec((8, 2, XR, K, LY), lambda i: (i, 0, 0, 0, 0))
     return pl.pallas_call(
         basis_kernel,
         out_shape=(jax.ShapeDtypeStruct((1, 2 * K, 2, LX, LY), F32), jax.ShapeDtypeStruct((1, 64, 64), F32)),
-        grid=(NC // 4,),
+        grid=(NC // 8,),
         in_specs=[pl.BlockSpec((64, 64), lambda i: (0, 0)), small, half, half],
-        out_specs=(pl.BlockSpec((1, 2 * K, 2, 4 * XR, LY), lambda i: (0, 0, 0, i, 0)), small),
+        out_specs=(pl.BlockSpec((1, 2 * K, 2, 8 * XR, LY), lambda i: (0, 0, 0, i, 0)), small),
         scratch_shapes=[pltpu.VMEM((XR, 2 * K, LY), F32)],
         compiler_params=pltpu.CompilerParams(vmem_limit_bytes=60 << 20),
         name="basis",

time: 220 us -> 219 us (level)
  no operation moved by 1% of the time
where the time goes in v4:
time: 219 us
  Pallas kernels  217 us (99%)
    pallas_call x1, Pallas kernels, run_filter(): pl.pallas_call(filter_kernel, out_shape=(jax.ShapeDtypeStruct((NC, 2, XR,...  209 us
    pallas_call x1, Pallas kernels, run_basis(): pl.pallas_call(basis_kernel, out_shape=(jax.ShapeDtypeStruct((1, 2 * K, 2...  7.9 us

profile of v4, /device:TPU:9, one launch (start us, length us, event | category | flops | bytes accessed | tf_op | source)
XLA Modules:
  0.0 219.0 jit_solution(13225569162994773552)
XLA Ops:
  1.9 209.1 %filter.1 = (f32[16,2,8,32,128]{4,3,2,1,0:T(8,128)}, f32[16,2,8,32,128]{4,3,2,1,0:T(8,128)}, f32[64,64]{1,0:T(8,128)}, f32[1,64,64]{2,1,0:T(8,128)}) custom-call(f32[32,2,128,128]{3,2,1,0:T(8,128)} %bitcast.1, f32[2,128,128]{2,1,0:T(8,128)} %on_hbm.1, f32[1]{0:T(128)S(6)} %copy.7.ctr_ref, f32[1]{0:T(128)S(6)} %copy.8.ih_ref, f32[1,3]{1,0:T(1,128)} %cheb.1), custom_call_target="tpu_custom_call" | custom-call | tf_op jit(solution)/shard_map/filter/pallas_call | solution.py:417
  211.1 7.9 %basis.1 = (f32[1,64,2,128,128]{4,3,2,1,0:T(8,128)}, f32[1,64,64]{2,1,0:T(8,128)}) custom-call(f32[64,64]{1,0:T(8,128)} %get-tuple-element.6.linv_ref, f32[1,64,64]{2,1,0:T(8,128)} %get-tuple-element.7.p_ref, f32[16,2,8,32,128]{4,3,2,1,0:T(8,128)} %get-tuple-element.8.f_ref, f32[16,2,8,32,128]{4,3,2,1,0:T(8,128)} %get-tuple-element.9.g_ref), custom_call_target="tpu_custom_call" | custom-call | tf_op jit(solution)/shard_map/basis/pallas_call | solution.py:479
